TPU v7x, 128 devices: a whole 4x4x4 slice. The times are simulated.
128 devices in a mesh: dom: 16 (over y_lo, z, core), rep: 8 (over y_hi, x).
Axes of the slice: x: 4, y: 4 (y_hi: 2, y_lo: 2; y = y_hi * 2 + y_lo), z: 4, core: 2. Of those that a mesh axis runs over, the one named last changes fastest.
Arguments:
- node_features: bfloat16 [65536, 256], P(('dom', 'rep')), may hold values from -6 to 6
- weight: bfloat16 [256, 256], replicated, may hold values from -0.375 to 0.375
- cotangent: bfloat16 [65536, 256], P(('dom', 'rep')), may hold values from -6 to 6
- tile_row: int32 [16, 8, 512], P('dom', 'rep'), may hold values from 0 to 31
- tile_col: int32 [16, 8, 512], P('dom', 'rep'), may hold values from 0 to 63
- tile_values: bfloat16 [16, 8, 512, 128, 128], P('dom', 'rep'), may hold values from -0.0625 to 0.0625
- tile_count: int32 [16, 8], P('dom', 'rep'), may hold values from 128 to 512, as said below
Outputs:
- output: bfloat16 [65536, 256], P(('dom', 'rep'))
- grad_features: bfloat16 [65536, 256], P(('dom', 'rep'))
- grad_weight: float32 [256, 256], replicated
Inputs may be any that keep to these rules, and one draw needn't show every extreme that they name: Live slots are the first tile_count slots of each device's list; some device has all 512 slots live.
All inputs are finite; a program needn't handle non-finite values.
Results may differ from a plain program's by a relative error of at most 0.0061.
Values may be sent and summed in bfloat16 or wider, within the bound.
No kernel may reach another device: no remote copies, remote signals or barrier semaphores. Data moves between devices by JAX's collectives and lax.ppermute only.
A program may use at most 192 MiB of HBM per device.

v0:
```python
import jax
import jax.numpy as jnp
from jax import lax
from jax.sharding import PartitionSpec as P


def silu_slope(summed):
    sig = jax.nn.sigmoid(summed)
    return sig * (1.0 + summed * (1.0 - sig))


def tile_products(values, pick_index, place_index, active, source, out_blocks, flipped):
    slots = values.shape[0]
    feature_width = source.shape[2]
    per_turn = min(slots, 128)
    pattern = "tba,tbf->taf" if flipped else "tab,tbf->taf"

    def accumulate(turn_index, summed):
        first_slot = turn_index * per_turn
        block_values = lax.dynamic_slice_in_dim(values, first_slot, per_turn, 0)
        picks = lax.dynamic_slice_in_dim(pick_index, first_slot, per_turn, 0)
        picked = jnp.take(source, picks, axis=0)
        products = jnp.einsum(pattern, block_values, picked, preferred_element_type=jnp.float32)
        places = lax.dynamic_slice_in_dim(place_index, first_slot, per_turn, 0)
        enabled = lax.dynamic_slice_in_dim(active, first_slot, per_turn, 0)
        products = products * enabled.astype(jnp.float32)[:, None, None]
        return summed.at[places].add(products)

    initial = jnp.zeros((out_blocks, 128, feature_width), jnp.float32)
    summed = lax.fori_loop(0, slots // per_turn, accumulate, initial)
    return summed.reshape(out_blocks * 128, feature_width)


def body(node_features, weight, cotangent, tile_row, tile_col, tile_values, tile_count):
    rows_here = node_features.shape[0]
    feature_width = weight.shape[0]
    dom_size = lax.axis_size("dom")
    rep_size = lax.axis_size("rep")
    slots = tile_row.shape[2]
    row_index = tile_row.reshape(slots)
    col_index = tile_col.reshape(slots)
    values = tile_values.reshape(slots, 128, 128)
    active = lax.broadcasted_iota(jnp.int32, (slots,), 0) < tile_count.reshape(())
    projected = jnp.dot(node_features, weight, preferred_element_type=jnp.float32).astype(
        jnp.bfloat16
    )
    gathered = lax.all_gather(projected, "dom", axis=0, tiled=True)
    source = gathered.reshape(-1, 128, feature_width)
    part_blocks = rep_size * rows_here // 128
    partial_value = tile_products(values, col_index, row_index, active, source, part_blocks, False)
    summed = lax.psum_scatter(partial_value, "rep", scatter_dimension=0, tiled=True)
    output = jax.nn.silu(summed).astype(jnp.bfloat16)
    grad_own = (cotangent.astype(jnp.float32) * silu_slope(summed)).astype(jnp.bfloat16)
    grad_block = lax.all_gather(grad_own, "rep", axis=0, tiled=True)
    back_blocks = dom_size * rows_here // 128
    back_partial = tile_products(
        values,
        row_index,
        col_index,
        active,
        grad_block.reshape(-1, 128, feature_width),
        back_blocks,
        True,
    )
    grad_projected = lax.psum_scatter(back_partial, "dom", scatter_dimension=0, tiled=True).astype(
        jnp.bfloat16
    )
    grad_features = jnp.dot(grad_projected, weight.T, preferred_element_type=jnp.float32).astype(
        jnp.bfloat16
    )
    local_weight = jnp.dot(node_features.T, grad_projected, preferred_element_type=jnp.float32)
    grad_weight = lax.psum(local_weight, ("dom", "rep"))
    return (output, grad_features, grad_weight)


def solution(mesh):
    placed = (
        P(("dom", "rep"), None),
        P(),
        P(("dom", "rep"), None),
        P("dom", "rep", None),
        P("dom", "rep", None),
        P("dom", "rep", None, None, None),
        P("dom", "rep"),
    )
    return jax.shard_map(
        body,
        mesh=mesh,
        in_specs=placed,
        out_specs=(P(("dom", "rep"), None), P(("dom", "rep"), None), P()),
        check_vma=False,
    )
```

profile of v0, /device:TPU:1, one launch (start us, length us, event | category | flops | bytes accessed | tf_op | source)
XLA Modules:
  0.0 908.0 jit_solution(10777865380881318707)
XLA Ops:
  7.2 0.9 copy-done
  8.1 1.8 convolution_convert_fusion.1
  10.7 40.7 %all-gather.3.cloned.1.call-done = bf16[8192,256]{1,0:T(8,128)(2,1)} async-done(((bf16[512,256]{1,0:T(8,128)(2,1)}), bf16[8192,256]{1,0:T(8,128)(2,1)}) %all-gather.3.cloned.1.call-update) | async-done | bytes 4194320 | tf_op jit(solution)/shard_map/all_gather | solution.py:47
  51.4 2.4 broadcast_in_dim.74
  53.8 244.2 %while.26 = (s32[]{:T(128)}, f32[32,128,256]{2,1,0:T(8,128)}, s32[512]{0:T(512)}, bf16[512,128,128]{2,1,0:T(8,128)(2,1)}, s32[512]{0:T(512)}, /*index=5*/bf16[64...) while((s32[]{:T(128)}, f32[32,128,256]{2,1,0:T(8,128)}, ...), condition=%wide.region_2.3_spmd, body=%wide.region_0.2_spmd.sunk | while | flops 1086327040 | bytes 96478248 | solution.py:30
  53.8 0.8 compare_and_fusion.4
  54.6 8.8 gather_fusion
  63.4 12.8 %convolution_multiply_fusion.4 = f32[128,128,256]{2,1,0:T(8,128)} fusion(f32[128]{0:T(128)S(1)} %get-tuple-element.384, bf16[128,128,256]{2,1,0:T(8,128)(2,1)} %gather_fusion, pred[128]{0:T(512)(128)(4,1)S(1)} %get-tuple-element.386, bf16[512,128,128]{2,1,0:T(8,128)(2,1)} %get-tuple-element.422, s32[]{:T(128)S(6)} %select_n.85), kind=kOutput, calls=%fused_computation.4.clone.1 | convolution fusion | flops 1082130432 | bytes 29360772 | tf_op jit(solution)/shard_map/while/body/eval_jaxpr/tab,tbf->taf/dot_general | solution.py:23
  76.9 38.1 %scatter_fusion = f32[32,128,256]{2,1,0:T(8,128)} fusion(f32[32,128,256]{2,1,0:T(8,128)} %get-tuple-element.409, s32[128]{0:T(128)S(1)} %compare_select_fusion.8, f32[128,128,256]{2,1,0:T(8,128)} %convolution_multiply_fusion.4), kind=kCustom, calls=%fused_computation.2.clone.1 | custom fusion | flops 4194304 | bytes 50332160 | tf_op jit(solution)/shard_map/while/body/eval_jaxpr/scatter-add | solution.py:27
  115.0 0.8 compare_and_fusion.4
  115.8 8.8 gather_fusion
  124.5 12.8 %convolution_multiply_fusion.4 = f32[128,128,256]{2,1,0:T(8,128)} fusion(f32[128]{0:T(128)S(1)} %get-tuple-element.384, bf16[128,128,256]{2,1,0:T(8,128)(2,1)} %gather_fusion, pred[128]{0:T(512)(128)(4,1)S(1)} %get-tuple-element.386, bf16[512,128,128]{2,1,0:T(8,128)(2,1)} %get-tuple-element.422, s32[]{:T(128)S(6)} %select_n.85), kind=kOutput, calls=%fused_computation.4.clone.1 | convolution fusion | flops 1082130432 | bytes 29360772 | tf_op jit(solution)/shard_map/while/body/eval_jaxpr/tab,tbf->taf/dot_general | solution.py:23
  138.1 38.1 %scatter_fusion = f32[32,128,256]{2,1,0:T(8,128)} fusion(f32[32,128,256]{2,1,0:T(8,128)} %get-tuple-element.409, s32[128]{0:T(128)S(1)} %compare_select_fusion.8, f32[128,128,256]{2,1,0:T(8,128)} %convolution_multiply_fusion.4), kind=kCustom, calls=%fused_computation.2.clone.1 | custom fusion | flops 4194304 | bytes 50332160 | tf_op jit(solution)/shard_map/while/body/eval_jaxpr/scatter-add | solution.py:27
  176.2 0.8 compare_and_fusion.4
  176.9 8.8 gather_fusion
  185.7 12.8 %convolution_multiply_fusion.4 = f32[128,128,256]{2,1,0:T(8,128)} fusion(f32[128]{0:T(128)S(1)} %get-tuple-element.384, bf16[128,128,256]{2,1,0:T(8,128)(2,1)} %gather_fusion, pred[128]{0:T(512)(128)(4,1)S(1)} %get-tuple-element.386, bf16[512,128,128]{2,1,0:T(8,128)(2,1)} %get-tuple-element.422, s32[]{:T(128)S(6)} %select_n.85), kind=kOutput, calls=%fused_computation.4.clone.1 | convolution fusion | flops 1082130432 | bytes 29360772 | tf_op jit(solution)/shard_map/while/body/eval_jaxpr/tab,tbf->taf/dot_general | solution.py:23
  199.3 37.7 %scatter_fusion = f32[32,128,256]{2,1,0:T(8,128)} fusion(f32[32,128,256]{2,1,0:T(8,128)} %get-tuple-element.409, s32[128]{0:T(128)S(1)} %compare_select_fusion.8, f32[128,128,256]{2,1,0:T(8,128)} %convolution_multiply_fusion.4), kind=kCustom, calls=%fused_computation.2.clone.1 | custom fusion | flops 4194304 | bytes 50332160 | tf_op jit(solution)/shard_map/while/body/eval_jaxpr/scatter-add | solution.py:27
  237.0 0.8 compare_and_fusion.4
  237.7 8.8 gather_fusion
  246.5 12.8 %convolution_multiply_fusion.4 = f32[128,128,256]{2,1,0:T(8,128)} fusion(f32[128]{0:T(128)S(1)} %get-tuple-element.384, bf16[128,128,256]{2,1,0:T(8,128)(2,1)} %gather_fusion, pred[128]{0:T(512)(128)(4,1)S(1)} %get-tuple-element.386, bf16[512,128,128]{2,1,0:T(8,128)(2,1)} %get-tuple-element.422, s32[]{:T(128)S(6)} %select_n.85), kind=kOutput, calls=%fused_computation.4.clone.1 | convolution fusion | flops 1082130432 | bytes 29360772 | tf_op jit(solution)/shard_map/while/body/eval_jaxpr/tab,tbf->taf/dot_general | solution.py:23
  260.1 37.9 %scatter_fusion = f32[32,128,256]{2,1,0:T(8,128)} fusion(f32[32,128,256]{2,1,0:T(8,128)} %get-tuple-element.409, s32[128]{0:T(128)S(1)} %compare_select_fusion.8, f32[128,128,256]{2,1,0:T(8,128)} %convolution_multiply_fusion.4), kind=kCustom, calls=%fused_computation.2.clone.1 | custom fusion | flops 4194304 | bytes 50332160 | tf_op jit(solution)/shard_map/while/body/eval_jaxpr/scatter-add | solution.py:27
  298.0 83.2 %reduce-scatter.3.cloned.1.call-done = f32[512,256]{1,0:T(8,128)} async-done(((f32[4096,256]{1,0:T(8,128)}), f32[512,256]{1,0:T(8,128)}) %reduce-scatter.3.cloned.1.call-update) | async-done | bytes 524304 | tf_op jit(solution)/shard_map/reduce_scatter | solution.py:51
  381.3 2.1 multiply_convert_fusion
  383.6 22.4 %copy.10 = bf16[1,1,512,128,128]{3,4,2,1,0:T(8,128)(2,1)} copy(bf16[1,1,512,128,128]{4,3,2,1,0:T(8,128)(2,1)} %bitcast.21) | data formatting | bytes 33554432 | tf_op args[5]
  406.0 31.9 %all-gather.5.cloned.1.call-done = bf16[4096,256]{1,0:T(8,128)(2,1)} async-done(((bf16[512,256]{1,0:T(8,128)(2,1)}), bf16[4096,256]{1,0:T(8,128)(2,1)}) %all-gather.5.cloned.1.call-update) | async-done | bytes 2097168 | tf_op jit(solution)/shard_map/all_gather | solution.py:54
  437.9 4.2 broadcast_in_dim.75
  442.1 236.8 %while.27 = (s32[]{:T(128)}, f32[64,128,256]{2,1,0:T(8,128)}, s32[512]{0:T(512)}, bf16[512,128,128]{1,2,0:T(8,128)(2,1)}, s32[512]{0:T(512)}, /*index=5*/bf16[32...) while((s32[]{:T(128)}, f32[64,128,256]{2,1,0:T(8,128)}, ...), condition=%wide.region_6.7_spmd, body=%wide.region_4.6_spmd.sunk | while | flops 1086327040 | bytes 96478248 | solution.py:30
  442.1 0.8 compare_and_fusion.5
  442.9 6.6 gather_fusion.1
  449.5 12.8 %convolution_multiply_fusion.5 = f32[128,128,256]{2,1,0:T(8,128)} fusion(f32[128]{0:T(128)S(1)} %get-tuple-element.394, bf16[128,128,256]{2,1,0:T(8,128)(2,1)} %gather_fusion.1, pred[128]{0:T(512)(128)(4,1)S(1)} %get-tuple-element.396, bf16[512,128,128]{1,2,0:T(8,128)(2,1)} %get-tuple-element.455, s32[]{:T(128)S(6)} %select_n.88), kind=kOutput, calls=%fused_computation.16.clone.1 | convolution fusion | flops 1082130432 | bytes 29360772 | tf_op jit(solution)/shard_map/while/body/eval_jaxpr/tba,tbf->taf/dot_general | solution.py:23
  463.1 38.5 %scatter_fusion.1 = f32[64,128,256]{2,1,0:T(8,128)} fusion(f32[64,128,256]{2,1,0:T(8,128)} %get-tuple-element.442, s32[128]{0:T(128)S(1)} %compare_select_fusion.9, f32[128,128,256]{2,1,0:T(8,128)} %convolution_multiply_fusion.5), kind=kCustom, calls=%fused_computation.3.clone.1 | custom fusion | flops 4194304 | bytes 50332160 | tf_op jit(solution)/shard_map/while/body/eval_jaxpr/scatter-add | solution.py:27
  501.6 0.8 compare_and_fusion.5
  502.3 6.6 gather_fusion.1
  508.9 12.8 %convolution_multiply_fusion.5 = f32[128,128,256]{2,1,0:T(8,128)} fusion(f32[128]{0:T(128)S(1)} %get-tuple-element.394, bf16[128,128,256]{2,1,0:T(8,128)(2,1)} %gather_fusion.1, pred[128]{0:T(512)(128)(4,1)S(1)} %get-tuple-element.396, bf16[512,128,128]{1,2,0:T(8,128)(2,1)} %get-tuple-element.455, s32[]{:T(128)S(6)} %select_n.88), kind=kOutput, calls=%fused_computation.16.clone.1 | convolution fusion | flops 1082130432 | bytes 29360772 | tf_op jit(solution)/shard_map/while/body/eval_jaxpr/tba,tbf->taf/dot_general | solution.py:23
  522.5 38.1 %scatter_fusion.1 = f32[64,128,256]{2,1,0:T(8,128)} fusion(f32[64,128,256]{2,1,0:T(8,128)} %get-tuple-element.442, s32[128]{0:T(128)S(1)} %compare_select_fusion.9, f32[128,128,256]{2,1,0:T(8,128)} %convolution_multiply_fusion.5), kind=kCustom, calls=%fused_computation.3.clone.1 | custom fusion | flops 4194304 | bytes 50332160 | tf_op jit(solution)/shard_map/while/body/eval_jaxpr/scatter-add | solution.py:27
  560.6 0.8 compare_and_fusion.5
  561.3 6.6 gather_fusion.1
  567.9 12.8 %convolution_multiply_fusion.5 = f32[128,128,256]{2,1,0:T(8,128)} fusion(f32[128]{0:T(128)S(1)} %get-tuple-element.394, bf16[128,128,256]{2,1,0:T(8,128)(2,1)} %gather_fusion.1, pred[128]{0:T(512)(128)(4,1)S(1)} %get-tuple-element.396, bf16[512,128,128]{1,2,0:T(8,128)(2,1)} %get-tuple-element.455, s32[]{:T(128)S(6)} %select_n.88), kind=kOutput, calls=%fused_computation.16.clone.1 | convolution fusion | flops 1082130432 | bytes 29360772 | tf_op jit(solution)/shard_map/while/body/eval_jaxpr/tba,tbf->taf/dot_general | solution.py:23
  581.5 38.3 %scatter_fusion.1 = f32[64,128,256]{2,1,0:T(8,128)} fusion(f32[64,128,256]{2,1,0:T(8,128)} %get-tuple-element.442, s32[128]{0:T(128)S(1)} %compare_select_fusion.9, f32[128,128,256]{2,1,0:T(8,128)} %convolution_multiply_fusion.5), kind=kCustom, calls=%fused_computation.3.clone.1 | custom fusion | flops 4194304 | bytes 50332160 | tf_op jit(solution)/shard_map/while/body/eval_jaxpr/scatter-add | solution.py:27
  619.8 0.8 compare_and_fusion.5
  620.5 6.6 gather_fusion.1
  627.1 12.8 %convolution_multiply_fusion.5 = f32[128,128,256]{2,1,0:T(8,128)} fusion(f32[128]{0:T(128)S(1)} %get-tuple-element.394, bf16[128,128,256]{2,1,0:T(8,128)(2,1)} %gather_fusion.1, pred[128]{0:T(512)(128)(4,1)S(1)} %get-tuple-element.396, bf16[512,128,128]{1,2,0:T(8,128)(2,1)} %get-tuple-element.455, s32[]{:T(128)S(6)} %select_n.88), kind=kOutput, calls=%fused_computation.16.clone.1 | convolution fusion | flops 1082130432 | bytes 29360772 | tf_op jit(solution)/shard_map/while/body/eval_jaxpr/tba,tbf->taf/dot_general | solution.py:23
  640.7 38.3 %scatter_fusion.1 = f32[64,128,256]{2,1,0:T(8,128)} fusion(f32[64,128,256]{2,1,0:T(8,128)} %get-tuple-element.442, s32[128]{0:T(128)S(1)} %compare_select_fusion.9, f32[128,128,256]{2,1,0:T(8,128)} %convolution_multiply_fusion.5), kind=kCustom, calls=%fused_computation.3.clone.1 | custom fusion | flops 4194304 | bytes 50332160 | tf_op jit(solution)/shard_map/while/body/eval_jaxpr/scatter-add | solution.py:27
  679.0 71.8 %reduce-scatter.5.cloned.1.call-done = f32[512,256]{1,0:T(8,128)} async-done(((f32[8192,256]{1,0:T(8,128)}), f32[512,256]{1,0:T(8,128)}) %reduce-scatter.5.cloned.1.call-update) | async-done | bytes 524304 | tf_op jit(solution)/shard_map/reduce_scatter | solution.py:65
  750.8 2.0 convolution_bitcast_fusion
  752.9 2.0 convolution_convert_fusion
  754.9 144.8 %all-reduce.2.cloned.1.call-done = f32[256,256]{0,1:T(8,128)} async-done(((f32[256,256]{0,1:T(8,128)}), f32[256,256]{0,1:T(8,128)}) %all-reduce.2.cloned.1.call-update) | async-done | bytes 262160 | tf_op jit(solution)/shard_map/psum | solution.py:72
  899.6 1.8 copy.12
  (34 shorter events, 6.6 us)
Async XLA Ops:
  7.2 1.0 copy-start
  7.2 44.2 %all-gather.3.cloned.1.call-start = ((), (), s32[]{:S(2)}) async-start(), calls=%async_computation.2 | async-start | bytes 4456448 | tf_op jit(solution)/shard_map/all_gather | solution.py:47
  10.0 371.3 %reduce-scatter.3.cloned.1.call-start = ((), (), s32[]{:S(2)}) async-start(), calls=%async_computation.3 | async-start | bytes 4718592 | tf_op jit(solution)/shard_map/reduce_scatter | solution.py:51
  53.8 327.5 %copy-start.3 = (bf16[512,256]{1,0:T(8,128)(2,1)S(1)}, bf16[512,256]{1,0:T(8,128)(2,1)}, u32[]{:S(2)}) copy-start(bf16[512,256]{1,0:T(8,128)(2,1)} %param.13) | copy-start | bytes 786436
  298.0 139.9 %all-gather.5.cloned.1.call-start = ((), (), s32[]{:S(2)}) async-start(), calls=%async_computation.4 | async-start | bytes 2359296 | tf_op jit(solution)/shard_map/all_gather | solution.py:54
  383.4 367.4 %reduce-scatter.5.cloned.1.call-start = ((), (), s32[]{:S(2)}) async-start(), calls=%async_computation.5 | async-start | bytes 8912896 | tf_op jit(solution)/shard_map/reduce_scatter | solution.py:65
  437.9 4.2 copy-start.1
  679.0 73.9 %copy-start.2 = (bf16[256,256]{1,0:T(8,128)(2,1)S(1)}, bf16[256,256]{1,0:T(8,128)(2,1)}, u32[]{:S(2)}) copy-start(bf16[256,256]{1,0:T(8,128)(2,1)} %param.12) | copy-start | bytes 393220
  679.0 220.6 %all-reduce.2.cloned.1.call-start = ((), (), s32[]{:S(2)}) async-start(), calls=%async_computation.6 | async-start | bytes 524288 | tf_op jit(solution)/shard_map/psum | solution.py:72
Sparse Core Ops, SparseCore 0:
  10.3 41.0 all-gather.2
  298.1 83.1 reduce-scatter.2
  384.2 53.6 all-gather.4
  679.1 71.6 reduce-scatter.4
  756.0 143.6 all-reduce.1
where the time goes:
time: 910 us; the launch traced here: 908 us
  waiting for transfers between devices  372 us (41%)
  other arithmetic  319 us (35%)
  matrix products  108 us (12%)
  local copies, waits for them, and re-layouts  93.1 us (10%)
  between operations  14.5 us (2%)
    scatter-add x8, other arithmetic, accumulate(): return summed.at[places].add(products)  305 us
    psum x1, waiting for transfers between devices, body(): grad_weight = lax.psum(local_weight, ('dom', 'rep'))  145 us
    dot_general x8, matrix products, accumulate(): jnp.einsum(pattern, block_values, picked, preferred_element_type=jnp.floa...  103 us
    reduce_scatter x1, waiting for transfers between devices, body(): lax.psum_scatter(partial_value, 'rep', scatter_dimension=0, tiled=True)  83.2 us
    reduce_scatter x1, waiting for transfers between devices, body(): lax.psum_scatter(back_partial, 'dom', scatter_dimension=0, tiled=True)  71.8 us
    gather x8, local copies, waits for them, and re-layouts, accumulate(): picked = jnp.take(source, picks, axis=0)  61.3 us
    all_gather x1, waiting for transfers between devices, body(): gathered = lax.all_gather(projected, 'dom', axis=0, tiled=True)  40.7 us
    all_gather x1, waiting for transfers between devices, body(): grad_block = lax.all_gather(grad_own, 'rep', axis=0, tiled=True)  31.9 us
  transfers between devices with their start and end apart: 5, of which 5 were waited for; matrix products, arithmetic and copies ran while one was open for 3% of the time, Pallas kernels for 0%

commit v1 on v0

--- a/solution.py
+++ b/solution.py
@@ -69,7 +69,7 @@
         jnp.bfloat16
     )
     local_weight = jnp.dot(node_features.T, grad_projected, preferred_element_type=jnp.float32)
-    grad_weight = lax.psum(local_weight, ("dom", "rep"))
+    grad_weight = lax.psum(lax.psum(local_weight, "rep"), "dom")
     return (output, grad_features, grad_weight)
 
 

time: 910 us -> 968 us (1.064)
  waiting for transfers between devices: 372 us -> 430 us
    psum x1 -> x2, waiting for transfers between devices: 145 us -> 202 us  [body(): grad_weight = lax.psum(lax.psum(local_weight, 'rep'), 'dom')]
  transfers between devices with their start and end apart: 5 -> 6, of which waited for: 5 -> 6; matrix products, arithmetic and copies ran while one was open for 3% -> 3% of each run, Pallas kernels for 0% -> 0%
where the time goes in v1:
time: 968 us; the launch traced here: 966 us
  waiting for transfers between devices  430 us (44%)
  other arithmetic  319 us (33%)
  matrix products  108 us (11%)
  local copies, waits for them, and re-layouts  93.1 us (10%)
  between operations  14.8 us (2%)
    scatter-add x8, other arithmetic, accumulate(): return summed.at[places].add(products)  305 us
    psum x2, waiting for transfers between devices, body(): grad_weight = lax.psum(lax.psum(local_weight, 'rep'), 'dom')  202 us
    dot_general x8, matrix products, accumulate(): jnp.einsum(pattern, block_values, picked, preferred_element_type=jnp.floa...  103 us
    reduce_scatter x1, waiting for transfers between devices, body(): lax.psum_scatter(partial_value, 'rep', scatter_dimension=0, tiled=True)  83.2 us
    reduce_scatter x1, waiting for transfers between devices, body(): lax.psum_scatter(back_partial, 'dom', scatter_dimension=0, tiled=True)  71.8 us
    gather x8, local copies, waits for them, and re-layouts, accumulate(): picked = jnp.take(source, picks, axis=0)  61.3 us
    all_gather x1, waiting for transfers between devices, body(): gathered = lax.all_gather(projected, 'dom', axis=0, tiled=True)  40.7 us
    all_gather x1, waiting for transfers between devices, body(): grad_block = lax.all_gather(grad_own, 'rep', axis=0, tiled=True)  31.9 us
  transfers between devices with their start and end apart: 6, of which 6 were waited for; matrix products, arithmetic and copies ran while one was open for 3% of the time, Pallas kernels for 0%

profile of v1, /device:TPU:1, one launch (start us, length us, event | category | flops | bytes accessed | tf_op | source)
XLA Modules:
  0.0 965.9 jit_solution(5782684220008788407)
XLA Ops:
  7.2 0.9 copy-done
  8.1 1.8 convolution_convert_fusion.1
  10.7 40.7 %all-gather.3.cloned.1.call-done = bf16[8192,256]{1,0:T(8,128)(2,1)} async-done(((bf16[512,256]{1,0:T(8,128)(2,1)}), bf16[8192,256]{1,0:T(8,128)(2,1)}) %all-gather.3.cloned.1.call-update) | async-done | bytes 4194320 | tf_op jit(solution)/shard_map/all_gather | solution.py:47
  51.4 2.4 broadcast_in_dim.74
  53.8 244.2 %while.26 = (s32[]{:T(128)}, f32[32,128,256]{2,1,0:T(8,128)}, s32[512]{0:T(512)}, bf16[512,128,128]{2,1,0:T(8,128)(2,1)}, s32[512]{0:T(512)}, /*index=5*/bf16[64...) while((s32[]{:T(128)}, f32[32,128,256]{2,1,0:T(8,128)}, ...), condition=%wide.region_2.3_spmd, body=%wide.region_0.2_spmd.sunk | while | flops 1086327040 | bytes 96478248 | solution.py:30
  53.8 0.8 compare_and_fusion.4
  54.6 8.8 gather_fusion
  63.4 12.8 %convolution_multiply_fusion.4 = f32[128,128,256]{2,1,0:T(8,128)} fusion(f32[128]{0:T(128)S(1)} %get-tuple-element.384, bf16[128,128,256]{2,1,0:T(8,128)(2,1)} %gather_fusion, pred[128]{0:T(512)(128)(4,1)S(1)} %get-tuple-element.386, bf16[512,128,128]{2,1,0:T(8,128)(2,1)} %get-tuple-element.422, s32[]{:T(128)S(6)} %select_n.85), kind=kOutput, calls=%fused_computation.4.clone.1 | convolution fusion | flops 1082130432 | bytes 29360772 | tf_op jit(solution)/shard_map/while/body/eval_jaxpr/tab,tbf->taf/dot_general | solution.py:23
  76.9 38.1 %scatter_fusion = f32[32,128,256]{2,1,0:T(8,128)} fusion(f32[32,128,256]{2,1,0:T(8,128)} %get-tuple-element.409, s32[128]{0:T(128)S(1)} %compare_select_fusion.8, f32[128,128,256]{2,1,0:T(8,128)} %convolution_multiply_fusion.4), kind=kCustom, calls=%fused_computation.2.clone.1 | custom fusion | flops 4194304 | bytes 50332160 | tf_op jit(solution)/shard_map/while/body/eval_jaxpr/scatter-add | solution.py:27
  115.0 0.8 compare_and_fusion.4
  115.8 8.8 gather_fusion
  124.5 12.8 %convolution_multiply_fusion.4 = f32[128,128,256]{2,1,0:T(8,128)} fusion(f32[128]{0:T(128)S(1)} %get-tuple-element.384, bf16[128,128,256]{2,1,0:T(8,128)(2,1)} %gather_fusion, pred[128]{0:T(512)(128)(4,1)S(1)} %get-tuple-element.386, bf16[512,128,128]{2,1,0:T(8,128)(2,1)} %get-tuple-element.422, s32[]{:T(128)S(6)} %select_n.85), kind=kOutput, calls=%fused_computation.4.clone.1 | convolution fusion | flops 1082130432 | bytes 29360772 | tf_op jit(solution)/shard_map/while/body/eval_jaxpr/tab,tbf->taf/dot_general | solution.py:23
  138.1 38.1 %scatter_fusion = f32[32,128,256]{2,1,0:T(8,128)} fusion(f32[32,128,256]{2,1,0:T(8,128)} %get-tuple-element.409, s32[128]{0:T(128)S(1)} %compare_select_fusion.8, f32[128,128,256]{2,1,0:T(8,128)} %convolution_multiply_fusion.4), kind=kCustom, calls=%fused_computation.2.clone.1 | custom fusion | flops 4194304 | bytes 50332160 | tf_op jit(solution)/shard_map/while/body/eval_jaxpr/scatter-add | solution.py:27
  176.2 0.8 compare_and_fusion.4
  176.9 8.8 gather_fusion
  185.7 12.8 %convolution_multiply_fusion.4 = f32[128,128,256]{2,1,0:T(8,128)} fusion(f32[128]{0:T(128)S(1)} %get-tuple-element.384, bf16[128,128,256]{2,1,0:T(8,128)(2,1)} %gather_fusion, pred[128]{0:T(512)(128)(4,1)S(1)} %get-tuple-element.386, bf16[512,128,128]{2,1,0:T(8,128)(2,1)} %get-tuple-element.422, s32[]{:T(128)S(6)} %select_n.85), kind=kOutput, calls=%fused_computation.4.clone.1 | convolution fusion | flops 1082130432 | bytes 29360772 | tf_op jit(solution)/shard_map/while/body/eval_jaxpr/tab,tbf->taf/dot_general | solution.py:23
  199.3 37.7 %scatter_fusion = f32[32,128,256]{2,1,0:T(8,128)} fusion(f32[32,128,256]{2,1,0:T(8,128)} %get-tuple-element.409, s32[128]{0:T(128)S(1)} %compare_select_fusion.8, f32[128,128,256]{2,1,0:T(8,128)} %convolution_multiply_fusion.4), kind=kCustom, calls=%fused_computation.2.clone.1 | custom fusion | flops 4194304 | bytes 50332160 | tf_op jit(solution)/shard_map/while/body/eval_jaxpr/scatter-add | solution.py:27
  237.0 0.8 compare_and_fusion.4
  237.7 8.8 gather_fusion
  246.5 12.8 %convolution_multiply_fusion.4 = f32[128,128,256]{2,1,0:T(8,128)} fusion(f32[128]{0:T(128)S(1)} %get-tuple-element.384, bf16[128,128,256]{2,1,0:T(8,128)(2,1)} %gather_fusion, pred[128]{0:T(512)(128)(4,1)S(1)} %get-tuple-element.386, bf16[512,128,128]{2,1,0:T(8,128)(2,1)} %get-tuple-element.422, s32[]{:T(128)S(6)} %select_n.85), kind=kOutput, calls=%fused_computation.4.clone.1 | convolution fusion | flops 1082130432 | bytes 29360772 | tf_op jit(solution)/shard_map/while/body/eval_jaxpr/tab,tbf->taf/dot_general | solution.py:23
  260.1 37.9 %scatter_fusion = f32[32,128,256]{2,1,0:T(8,128)} fusion(f32[32,128,256]{2,1,0:T(8,128)} %get-tuple-element.409, s32[128]{0:T(128)S(1)} %compare_select_fusion.8, f32[128,128,256]{2,1,0:T(8,128)} %convolution_multiply_fusion.4), kind=kCustom, calls=%fused_computation.2.clone.1 | custom fusion | flops 4194304 | bytes 50332160 | tf_op jit(solution)/shard_map/while/body/eval_jaxpr/scatter-add | solution.py:27
  298.0 83.2 %reduce-scatter.3.cloned.1.call-done = f32[512,256]{1,0:T(8,128)} async-done(((f32[4096,256]{1,0:T(8,128)}), f32[512,256]{1,0:T(8,128)}) %reduce-scatter.3.cloned.1.call-update) | async-done | bytes 524304 | tf_op jit(solution)/shard_map/reduce_scatter | solution.py:51
  381.3 2.1 multiply_convert_fusion
  383.6 22.4 %copy.10 = bf16[1,1,512,128,128]{3,4,2,1,0:T(8,128)(2,1)} copy(bf16[1,1,512,128,128]{4,3,2,1,0:T(8,128)(2,1)} %bitcast.21) | data formatting | bytes 33554432 | tf_op args[5]
  406.0 31.9 %all-gather.5.cloned.1.call-done = bf16[4096,256]{1,0:T(8,128)(2,1)} async-done(((bf16[512,256]{1,0:T(8,128)(2,1)}), bf16[4096,256]{1,0:T(8,128)(2,1)}) %all-gather.5.cloned.1.call-update) | async-done | bytes 2097168 | tf_op jit(solution)/shard_map/all_gather | solution.py:54
  437.9 4.2 broadcast_in_dim.75
  442.1 236.8 %while.27 = (s32[]{:T(128)}, f32[64,128,256]{2,1,0:T(8,128)}, s32[512]{0:T(512)}, bf16[512,128,128]{1,2,0:T(8,128)(2,1)}, s32[512]{0:T(512)}, /*index=5*/bf16[32...) while((s32[]{:T(128)}, f32[64,128,256]{2,1,0:T(8,128)}, ...), condition=%wide.region_6.7_spmd, body=%wide.region_4.6_spmd.sunk | while | flops 1086327040 | bytes 96478248 | solution.py:30
  442.1 0.8 compare_and_fusion.5
  442.9 6.6 gather_fusion.1
  449.5 12.8 %convolution_multiply_fusion.5 = f32[128,128,256]{2,1,0:T(8,128)} fusion(f32[128]{0:T(128)S(1)} %get-tuple-element.394, bf16[128,128,256]{2,1,0:T(8,128)(2,1)} %gather_fusion.1, pred[128]{0:T(512)(128)(4,1)S(1)} %get-tuple-element.396, bf16[512,128,128]{1,2,0:T(8,128)(2,1)} %get-tuple-element.455, s32[]{:T(128)S(6)} %select_n.88), kind=kOutput, calls=%fused_computation.16.clone.1 | convolution fusion | flops 1082130432 | bytes 29360772 | tf_op jit(solution)/shard_map/while/body/eval_jaxpr/tba,tbf->taf/dot_general | solution.py:23
  463.1 38.5 %scatter_fusion.1 = f32[64,128,256]{2,1,0:T(8,128)} fusion(f32[64,128,256]{2,1,0:T(8,128)} %get-tuple-element.442, s32[128]{0:T(128)S(1)} %compare_select_fusion.9, f32[128,128,256]{2,1,0:T(8,128)} %convolution_multiply_fusion.5), kind=kCustom, calls=%fused_computation.3.clone.1 | custom fusion | flops 4194304 | bytes 50332160 | tf_op jit(solution)/shard_map/while/body/eval_jaxpr/scatter-add | solution.py:27
  501.6 0.8 compare_and_fusion.5
  502.3 6.6 gather_fusion.1
  508.9 12.8 %convolution_multiply_fusion.5 = f32[128,128,256]{2,1,0:T(8,128)} fusion(f32[128]{0:T(128)S(1)} %get-tuple-element.394, bf16[128,128,256]{2,1,0:T(8,128)(2,1)} %gather_fusion.1, pred[128]{0:T(512)(128)(4,1)S(1)} %get-tuple-element.396, bf16[512,128,128]{1,2,0:T(8,128)(2,1)} %get-tuple-element.455, s32[]{:T(128)S(6)} %select_n.88), kind=kOutput, calls=%fused_computation.16.clone.1 | convolution fusion | flops 1082130432 | bytes 29360772 | tf_op jit(solution)/shard_map/while/body/eval_jaxpr/tba,tbf->taf/dot_general | solution.py:23
  522.5 38.1 %scatter_fusion.1 = f32[64,128,256]{2,1,0:T(8,128)} fusion(f32[64,128,256]{2,1,0:T(8,128)} %get-tuple-element.442, s32[128]{0:T(128)S(1)} %compare_select_fusion.9, f32[128,128,256]{2,1,0:T(8,128)} %convolution_multiply_fusion.5), kind=kCustom, calls=%fused_computation.3.clone.1 | custom fusion | flops 4194304 | bytes 50332160 | tf_op jit(solution)/shard_map/while/body/eval_jaxpr/scatter-add | solution.py:27
  561.3 6.6 gather_fusion.1
  567.9 12.8 %convolution_multiply_fusion.5 = f32[128,128,256]{2,1,0:T(8,128)} fusion(f32[128]{0:T(128)S(1)} %get-tuple-element.394, bf16[128,128,256]{2,1,0:T(8,128)(2,1)} %gather_fusion.1, pred[128]{0:T(512)(128)(4,1)S(1)} %get-tuple-element.396, bf16[512,128,128]{1,2,0:T(8,128)(2,1)} %get-tuple-element.455, s32[]{:T(128)S(6)} %select_n.88), kind=kOutput, calls=%fused_computation.16.clone.1 | convolution fusion | flops 1082130432 | bytes 29360772 | tf_op jit(solution)/shard_map/while/body/eval_jaxpr/tba,tbf->taf/dot_general | solution.py:23
  581.5 38.3 %scatter_fusion.1 = f32[64,128,256]{2,1,0:T(8,128)} fusion(f32[64,128,256]{2,1,0:T(8,128)} %get-tuple-element.442, s32[128]{0:T(128)S(1)} %compare_select_fusion.9, f32[128,128,256]{2,1,0:T(8,128)} %convolution_multiply_fusion.5), kind=kCustom, calls=%fused_computation.3.clone.1 | custom fusion | flops 4194304 | bytes 50332160 | tf_op jit(solution)/shard_map/while/body/eval_jaxpr/scatter-add | solution.py:27
  619.8 0.8 compare_and_fusion.5
  620.5 6.6 gather_fusion.1
  627.1 12.8 %convolution_multiply_fusion.5 = f32[128,128,256]{2,1,0:T(8,128)} fusion(f32[128]{0:T(128)S(1)} %get-tuple-element.394, bf16[128,128,256]{2,1,0:T(8,128)(2,1)} %gather_fusion.1, pred[128]{0:T(512)(128)(4,1)S(1)} %get-tuple-element.396, bf16[512,128,128]{1,2,0:T(8,128)(2,1)} %get-tuple-element.455, s32[]{:T(128)S(6)} %select_n.88), kind=kOutput, calls=%fused_computation.16.clone.1 | convolution fusion | flops 1082130432 | bytes 29360772 | tf_op jit(solution)/shard_map/while/body/eval_jaxpr/tba,tbf->taf/dot_general | solution.py:23
  640.7 38.3 %scatter_fusion.1 = f32[64,128,256]{2,1,0:T(8,128)} fusion(f32[64,128,256]{2,1,0:T(8,128)} %get-tuple-element.442, s32[128]{0:T(128)S(1)} %compare_select_fusion.9, f32[128,128,256]{2,1,0:T(8,128)} %convolution_multiply_fusion.5), kind=kCustom, calls=%fused_computation.3.clone.1 | custom fusion | flops 4194304 | bytes 50332160 | tf_op jit(solution)/shard_map/while/body/eval_jaxpr/scatter-add | solution.py:27
  679.1 71.8 %reduce-scatter.5.cloned.1.call-done = f32[512,256]{1,0:T(8,128)} async-done(((f32[8192,256]{1,0:T(8,128)}), f32[512,256]{1,0:T(8,128)}) %reduce-scatter.5.cloned.1.call-update) | async-done | bytes 524304 | tf_op jit(solution)/shard_map/reduce_scatter | solution.py:65
  750.8 2.0 convolution_bitcast_fusion
  752.9 81.8 %all-reduce.3.cloned.1.call-done = f32[256,256]{0,1:T(8,128)} async-done(((f32[256,256]{0,1:T(8,128)}), f32[256,256]{0,1:T(8,128)}) %all-reduce.3.cloned.1.call-update) | async-done | bytes 262160 | tf_op jit(solution)/shard_map/psum | solution.py:72
  834.7 2.0 convolution_convert_fusion
  836.8 120.5 %all-reduce.5.cloned.1.call-done = f32[256,256]{0,1:T(8,128)} async-done(((f32[256,256]{0,1:T(8,128)}), f32[256,256]{0,1:T(8,128)}) %all-reduce.5.cloned.1.call-update) | async-done | bytes 262160 | tf_op jit(solution)/shard_map/psum | solution.py:72
  957.2 1.8 copy.12
  (37 shorter events, 7.4 us)
Async XLA Ops:
  7.2 1.0 copy-start
  7.2 44.2 %all-gather.3.cloned.1.call-start = ((), (), s32[]{:S(2)}) async-start(), calls=%async_computation.2 | async-start | bytes 4456448 | tf_op jit(solution)/shard_map/all_gather | solution.py:47
  10.0 371.3 %reduce-scatter.3.cloned.1.call-start = ((), (), s32[]{:S(2)}) async-start(), calls=%async_computation.3 | async-start | bytes 4718592 | tf_op jit(solution)/shard_map/reduce_scatter | solution.py:51
  53.8 327.5 %copy-start.3 = (bf16[512,256]{1,0:T(8,128)(2,1)S(1)}, bf16[512,256]{1,0:T(8,128)(2,1)}, u32[]{:S(2)}) copy-start(bf16[512,256]{1,0:T(8,128)(2,1)} %param.13) | copy-start | bytes 786436
  298.0 139.9 %all-gather.5.cloned.1.call-start = ((), (), s32[]{:S(2)}) async-start(), calls=%async_computation.4 | async-start | bytes 2359296 | tf_op jit(solution)/shard_map/all_gather | solution.py:54
  383.4 367.4 %reduce-scatter.5.cloned.1.call-start = ((), (), s32[]{:S(2)}) async-start(), calls=%async_computation.5 | async-start | bytes 8912896 | tf_op jit(solution)/shard_map/reduce_scatter | solution.py:65
  437.9 4.2 copy-start.1
  679.0 155.8 %copy-start.2 = (bf16[256,256]{1,0:T(8,128)(2,1)S(1)}, bf16[256,256]{1,0:T(8,128)(2,1)}, u32[]{:S(2)}) copy-start(bf16[256,256]{1,0:T(8,128)(2,1)} %param.12) | copy-start | bytes 393220
  679.0 155.7 %all-reduce.3.cloned.1.call-start = ((), (), s32[]{:S(2)}) async-start(), calls=%async_computation.6 | async-start | bytes 524288 | tf_op jit(solution)/shard_map/psum | solution.py:72
  752.8 204.4 %all-reduce.5.cloned.1.call-start = ((), (), s32[]{:S(2)}) async-start(), calls=%async_computation.7 | async-start | bytes 524288 | tf_op jit(solution)/shard_map/psum | solution.py:72
Sparse Core Ops, SparseCore 0:
  10.3 41.0 all-gather.2
  298.1 83.1 reduce-scatter.2
  384.2 53.6 all-gather.4
  679.1 71.6 reduce-scatter.4
  753.7 80.9 all-reduce.2
  837.2 120.0 all-reduce.4
